TPU v7x, 256 devices: a whole 4x4x8 slice. The times are simulated.
256 devices in a mesh: rows: 8 (over y, core), chan: 32 (over x, z).
Axes of the slice: x: 4, y: 4, z: 8, core: 2. Of those that a mesh axis runs over, the one named last changes fastest.
Arguments:
- features: bfloat16 [512, 1536, 256], P('rows', 'chan'), may hold values from -6 to 6
- mixing: float32 [3, 512, 256], P(None, 'rows'), may hold values from 0 to 1, as said below
- decay_rate: float32 [512, 256], P('rows'), may hold values from 0 to 0.5, as said below
- gate_input: bfloat16 [512, 1536, 256], P('rows', 'chan'), may hold values from -6 to 6
- out_weight: bfloat16 [1536, 1536], replicated, may hold values from -0.15625 to 0.15625
Outputs:
- projected: bfloat16 [512, 1536, 256], P(('rows', 'chan'))
Inputs may be any that keep to these rules, and one draw needn't show every extreme that they name: `mixing`: at every row and column the three weights are positive where their neighbour exists, the left weight is zero at column 0 and the right weight at column 255, and the three sum to one. `decay_rate`: every entry is positive.
All inputs are finite; a program needn't handle non-finite values.
Results may differ from a plain program's by a relative error of at most 0.0049.
Values may be sent and summed in bfloat16 or wider, within the bound.
No kernel may reach another device: no remote copies, remote signals or barrier semaphores. Data moves between devices by JAX's collectives and lax.ppermute only.
A program may use at most 128 MiB of HBM per device.

v0:
```python
import jax
import jax.numpy as jnp
from jax import lax
from jax.sharding import PartitionSpec as P

BLOCK = 16


def entering(part, axis, combine, identity):
    place = lax.axis_index(axis)
    gathered = jax.tree.map(lambda a: lax.all_gather(a, axis), part)
    state = jax.tree.map(lambda a, e: jnp.zeros_like(a) + jnp.asarray(e, a.dtype), part, identity)

    def one(lap, state):
        return combine(
            state, jax.tree.map(lambda a: lax.dynamic_index_in_dim(a, lap, 0, False), gathered)
        )

    return lax.fori_loop(0, place, one, state)


def spread(current, left_w, mid_w, right_w):
    edge_col = jnp.zeros(current.shape[:-1] + (1,), current.dtype)
    before_col = jnp.concatenate([edge_col, current[..., :-1]], axis=-1)
    after_col = jnp.concatenate([current[..., 1:], edge_col], axis=-1)
    return left_w * before_col + mid_w * current + right_w * after_col


def shards(features, mixing, decay_rate, gate_input, out_weight):
    rows_here, channels, col_count = features.shape
    blocks = rows_here // BLOCK
    highest = lax.Precision.HIGHEST
    retain = 1.0 - decay_rate
    weights = retain[None] * mixing
    in_scale = jnp.sqrt(decay_rate)
    forcing = in_scale[:, None, :] * features.astype(jnp.float32)
    coef_steps = weights.reshape(3, blocks, BLOCK, col_count).transpose(2, 0, 1, 3)
    force_steps = forcing.reshape(blocks, BLOCK, channels, col_count).swapaxes(0, 1)
    identity_op = jnp.eye(col_count, dtype=jnp.float32)

    def advance(carry_pair, inputs):
        local_st, op_stack = carry_pair
        coef_row, push_row = inputs
        left_w = coef_row[0][:, None, :]
        mid_w = coef_row[1][:, None, :]
        right_w = coef_row[2][:, None, :]
        local_st = spread(local_st, left_w, mid_w, right_w) + push_row
        op_stack = spread(op_stack, left_w, mid_w, right_w)
        return ((local_st, op_stack), (local_st, op_stack))

    initial = (
        jnp.zeros((blocks, channels, col_count), jnp.float32),
        jnp.broadcast_to(identity_op, (blocks, col_count, col_count)),
    )
    _, (local_all, ops_all) = lax.scan(advance, initial, (coef_steps, force_steps))
    last_ops = ops_all[-1]
    last_local = local_all[-1]

    def carry_on(current, inputs):
        block_op, loc_end = inputs
        return (jnp.dot(current, block_op, precision=highest) + loc_end, current)

    def compose_ops(running, block_op):
        return (jnp.dot(running, block_op, precision=highest), running)

    summary, _ = lax.scan(compose_ops, identity_op, last_ops)
    zero_state = jnp.zeros((channels, col_count), jnp.float32)
    offset, _ = lax.scan(carry_on, zero_state, (last_ops, last_local))

    def compose(earlier, later_pair):
        return (
            jnp.dot(earlier[0], later_pair[0], precision=highest),
            jnp.dot(earlier[1], later_pair[0], precision=highest) + later_pair[1],
        )

    _, incoming = entering((summary, offset), "rows", compose, (identity_op, zero_state))
    _, starts = lax.scan(carry_on, incoming, (last_ops, last_local))
    states = local_all + jnp.einsum("bcv,jbvw->jbcw", starts, ops_all, precision=highest)
    states = states.swapaxes(0, 1).reshape(rows_here, channels, col_count)
    mixed_in = (states * jax.nn.silu(gate_input.astype(jnp.float32))).astype(jnp.bfloat16)
    return jnp.einsum(
        "oc,rcw->row",
        out_weight,
        lax.all_to_all(mixed_in, "chan", split_axis=0, concat_axis=1, tiled=True),
        preferred_element_type=jnp.float32,
    ).astype(jnp.bfloat16)


def solution(mesh):
    in_specs = (
        P("rows", "chan", None),
        P(None, "rows", None),
        P("rows", None),
        P("rows", "chan", None),
        P(),
    )
    out_specs = P(("rows", "chan"), None, None)
    return jax.shard_map(shards, mesh=mesh, in_specs=in_specs, out_specs=out_specs, check_vma=False)
```

profile of v0, /device:TPU:57, one launch (start us, length us, event | category | flops | bytes accessed | tf_op | source)
XLA Modules:
  0.0 202.0 jit_solution(2163504412927207205)
XLA Ops:
  7.6 3.5 %convert_multiply_fusion.1 = f32[64,48,256]{2,1,0:T(8,128)} fusion(bf16[64,48,256]{2,1,0:T(8,128)(2,1)} %param.15, f32[64,256]{1,0:T(8,128)S(1)} %get-tuple-element.273), kind=kLoop, calls=%fused_computation.46 | loop fusion | flops 1572864 | bytes 4784128 | tf_op jit(solution)/shard_map/mul | solution.py:36
  11.2 64.0 %while.65 = (s32[]{:T(128)}, f32[4,48,256]{2,1,0:T(8,128)S(1)}, f32[4,256,256]{2,1,0:T(8,128)S(1)}, f32[16,4,48,256]{3,2,1,0:T(8,128)}, f32[16,4,256,256]{3,2,1,...) while((s32[]{:T(128)}, f32[4,48,256]{2,1,0:T(8,128)S(1)}, ...), condition=%wide.region_1.2_spmd.clone, body=%wide.region_0.1_spmd.clone.sunk | while | flops 1703941 | bytes 11842204 | solution.py:55
  13.5 1.8 bitcast_dynamic-update-slice_fusion.7
  17.5 1.8 bitcast_dynamic-update-slice_fusion.7
  25.4 1.8 bitcast_dynamic-update-slice_fusion.7
  33.4 1.8 bitcast_dynamic-update-slice_fusion.7
  37.4 1.8 bitcast_dynamic-update-slice_fusion.7
  41.5 1.8 bitcast_dynamic-update-slice_fusion.7
  45.5 1.8 bitcast_dynamic-update-slice_fusion.7
  53.5 1.8 bitcast_dynamic-update-slice_fusion.7
  57.5 1.8 bitcast_dynamic-update-slice_fusion.7
  61.5 1.8 bitcast_dynamic-update-slice_fusion.7
  65.5 1.8 bitcast_dynamic-update-slice_fusion.7
  69.5 1.8 bitcast_dynamic-update-slice_fusion.7
  73.5 1.8 bitcast_dynamic-update-slice_fusion.7
  76.6 2.6 %while.62 = (s32[]{:T(128)}, f32[256,256]{0,1:T(8,128)S(1)}, f32[4,256,256]{2,1,0:T(8,128)S(1)}, s32[]{:T(128)}) while((s32[]{:T(128)}, f32[256,256]{0,1:T(8,128)S(1)}, f32[4,256,256]{2,1,0:T(8,128)S(1)}, s32[]{:T(128)}) %tuple.106), condition=%wide.region_3.4_spmd, body=%wide.region_2.3_spmd.sunk | while | flops 201326592 | bytes 1310777 | solution.py:66
  82.2 14.6 %all-gather.1 = f32[384,256]{1,0:T(8,128)} all-gather(f32[48,256]{1,0:T(8,128)S(1)} %get-tuple-element.156), channel_id=3, replica_groups=mesh['rows'=8,'chan'=32] {'rows'}, dimensions={0}, use_global_device_ids=true | all-gather | bytes 442368 | tf_op jit(solution)/shard_map/all_gather | solution.py:11
  96.7 12.7 %all-gather.4.cloned.1.call-done = f32[2048,256]{0,1:T(8,128)} async-done(((f32[256,256]{0,1:T(8,128)}), f32[2048,256]{0,1:T(8,128)}) %all-gather.4.cloned.1.call-update) | async-done | bytes 2097168 | tf_op jit(solution)/shard_map/all_gather | solution.py:11
  109.4 1.9 copy.23
  111.4 7.8 %while.63 = (s32[]{:T(128)}, f32[48,256]{1,0:T(8,128)S(1)}, s32[]{:T(128)}, f32[8,256,256]{2,1,0:T(8,128)S(1)}, f32[8,48,256]{2,1,0:T(8,128)}, /*index=5*/s32[]{:T(128)}, s32[]{:T(128)}, s32[]{:T(128)}) while((s32[]{:T(128)}, f32[48,256]{1,0:T(8,128)S(1)}, s32[]{:T(128)}, f32[8,256,256]{2,1,0:T(8,128)S(1)}, f32[8,48,256]{2,1,0:T(8,128)}, ...), condition=%wide.region_7.8_spmd, body=%wide.region_6.7_spmd.sunk | while | flops 37761028 | bytes 509047 | solution.py:19
  119.2 3.7 %while.64 = (s32[]{:T(128)}, f32[48,256]{1,0:T(8,128)S(1)}, f32[4,48,256]{2,1,0:T(8,128)}, f32[4,256,256]{2,1,0:T(8,128)S(1)}, f32[4,48,256]{2,1,0:T(8,128)S(1)}, /*index=5*/s32[]{:T(128)}) while((s32[]{:T(128)}, f32[48,256]{1,0:T(8,128)S(1)}, f32[4,48,256]{2,1,0:T(8,128)}, f32[4,256,256]{2,1,0:T(8,128)S(1)}, f32[4,48,256]{2,1,0:T(8,128)S(1)}, ...), condition=%wide.region_9.10_spmd, body=%wide.region_8.9_spmd.sunk | while | flops 37761024 | bytes 607813 | solution.py:77
  122.9 14.7 %bitcast_add_fusion.1 = f32[16,4,48,256]{3,2,0,1:T(8,128)S(1)} fusion(f32[16,4,48,256]{3,2,1,0:T(8,128)} %get-tuple-element.153, f32[16,4,256,256]{3,2,1,0:T(8,128)} %get-tuple-element.154, f32[4,48,256]{2,1,0:T(8,128)} %get-tuple-element.158), kind=kOutput, calls=%fused_computation.45 | convolution fusion | flops 2416705536 | bytes 23265280 | tf_op jit(solution)/shard_map/bcv,jbvw->jbcw/dot_general | solution.py:78
  138.7 49.8 %all_to_all.18 = bf16[64,48,256]{2,1,0:T(8,128)(2,1)S(1)} all-to-all(bf16[64,48,256]{2,1,0:T(8,128)(2,1)S(1)} %fusion.27), channel_id=1, replica_groups=mesh['rows'=8,'chan'=32] {'chan'}, dimensions={0} | all-to-all | bytes 3145728 | tf_op jit(solution)/shard_map/all_to_all | solution.py:84
  188.6 5.0 %fusion.31 = bf16[2,1536,256]{1,2,0:T(8,128)(2,1)S(1)} fusion(bf16[2,1536,256]{2,1,0:T(8,128)(2,1)S(1)} %bitcast.133, bf16[1536,1536]{1,0:T(8,128)(2,1)} %param.19), kind=kOutput, calls=%fused_computation.49 | convolution fusion | flops 2416705536 | bytes 7864320 | tf_op jit(solution)/shard_map/oc,rcw->row/dot_general | solution.py:81
  (182 shorter events, 63.1 us)
Async XLA Ops:
  6.5 4.6 %copy-start.2 = (f32[3,64,256]{2,1,0:T(8,128)S(1)}, f32[3,64,256]{2,1,0:T(8,128)}, u32[]{:S(2)}) copy-start(f32[3,64,256]{2,1,0:T(8,128)} %param.16) | copy-start | bytes 589828
  6.5 102.9 %all-gather.4.cloned.1.call-start = ((), (), s32[]{:S(2)}) async-start(), calls=%async_computation.1 | async-start | bytes 2359296 | tf_op jit(solution)/shard_map/all_gather | solution.py:11
  79.2 0.7 copy-start
  122.9 14.7 %copy-start.1 = (bf16[64,48,256]{2,1,0:T(8,128)(2,1)S(1)}, bf16[64,48,256]{2,1,0:T(8,128)(2,1)}, u32[]{:S(2)}) copy-start(bf16[64,48,256]{2,1,0:T(8,128)(2,1)} %param.18) | copy-start | bytes 4718596
Sparse Core Ops, SparseCore 0:
  80.1 29.3 all-gather.3
where the time goes:
time: 203 us; the launch traced here: 202 us
  blocking collectives  64.3 us (32%)
  other arithmetic  61.3 us (30%)
  matrix products  31.8 us (16%)
  local copies, waits for them, and re-layouts  17.2 us (8%)
  between operations  13.6 us (7%)
  waiting for transfers between devices  12.7 us (6%)
    dynamic_update_slice x32, other arithmetic, shards(): lax.scan(advance, initial, (coef_steps, force_steps))  55.5 us
    all_to_all x1, blocking collectives, shards(): lax.all_to_all(mixed_in, 'chan', split_axis=0, concat_axis=1, tiled=True)  49.8 us
    dot_general x1, matrix products, shards(): jnp.einsum('bcv,jbvw->jbcw', starts, ops_all, precision=highest)  14.7 us
    all_gather x1, blocking collectives, entering(): gathered = jax.tree.map(lambda a: lax.all_gather(a, axis), part)  14.6 us
    all_gather x1, waiting for transfers between devices, entering(): gathered = jax.tree.map(lambda a: lax.all_gather(a, axis), part)  12.7 us
    dot_general x7, matrix products, compose(): jnp.dot(earlier[1], later_pair[0], precision=highest) + later_pair[1]  7.51 us
    slice x32, local copies, waits for them, and re-layouts, spread(): before_col = jnp.concatenate([edge_col, current[..., :-1]], axis=-1)  7.43 us
    dot_general x1, matrix products, shards(): jnp.einsum('oc,rcw->row', out_weight, lax.all_to_all(mixed_in, 'chan', sp...  4.99 us
  transfers between devices with their start and end apart: 1, of which 1 were waited for; matrix products, arithmetic and copies ran while one was open for 1% of the time, Pallas kernels for 0%

commit v1 on v0

--- a/solution.py
+++ b/solution.py
@@ -81,7 +81,12 @@
     return jnp.einsum(
         "oc,rcw->row",
         out_weight,
-        lax.all_to_all(mixed_in, "chan", split_axis=0, concat_axis=1, tiled=True),
+        jnp.concatenate(
+            lax.all_to_all(
+                jnp.stack(jnp.split(mixed_in, lax.axis_size("chan"), axis=0)), "chan", 0, 0
+            ),
+            axis=1,
+        ),
         preferred_element_type=jnp.float32,
     ).astype(jnp.bfloat16)
 

time: 203 us -> 201 us (level)
  matrix products: 31.8 us -> 29.4 us
    dot_general x1, matrix products: 4.99 us -> 2.65 us  [shards(): jnp.einsum('oc,rcw->row', out_weight, jnp.concatenate(lax.all_to_all(jnp....]
where the time goes in v1:
time: 201 us; the launch traced here: 200 us
  blocking collectives  64.3 us (32%)
  other arithmetic  61.3 us (30%)
  matrix products  29.4 us (15%)
  local copies, waits for them, and re-layouts  17.3 us (9%)
  between operations  13.9 us (7%)
  waiting for transfers between devices  12.7 us (6%)
    dynamic_update_slice x32, other arithmetic, shards(): lax.scan(advance, initial, (coef_steps, force_steps))  55.5 us
    all_to_all x1, blocking collectives, shards(): lax.all_to_all(jnp.stack(jnp.split(mixed_in, lax.axis_size('chan'), axis=...  49.8 us
    dot_general x1, matrix products, shards(): jnp.einsum('bcv,jbvw->jbcw', starts, ops_all, precision=highest)  14.7 us
    all_gather x1, blocking collectives, entering(): gathered = jax.tree.map(lambda a: lax.all_gather(a, axis), part)  14.6 us
    all_gather x1, waiting for transfers between devices, entering(): gathered = jax.tree.map(lambda a: lax.all_gather(a, axis), part)  12.7 us
    dot_general x7, matrix products, compose(): jnp.dot(earlier[1], later_pair[0], precision=highest) + later_pair[1]  7.51 us
    slice x32, local copies, waits for them, and re-layouts, spread(): before_col = jnp.concatenate([edge_col, current[..., :-1]], axis=-1)  7.43 us
  transfers between devices with their start and end apart: 1, of which 1 were waited for; matrix products, arithmetic and copies ran while one was open for 1% of the time, Pallas kernels for 0%

profile of v1, /device:TPU:57, one launch (start us, length us, event | category | flops | bytes accessed | tf_op | source)
XLA Modules:
  0.0 200.2 jit_solution(16299586019483769999)
XLA Ops:
  7.6 3.5 %convert_multiply_fusion.1 = f32[64,48,256]{2,1,0:T(8,128)} fusion(bf16[64,48,256]{2,1,0:T(8,128)(2,1)} %param.15, f32[64,256]{1,0:T(8,128)S(1)} %get-tuple-element.273), kind=kLoop, calls=%fused_computation.46 | loop fusion | flops 1572864 | bytes 4784128 | tf_op jit(solution)/shard_map/mul | solution.py:36
  11.3 64.0 %while.65 = (s32[]{:T(128)}, f32[4,48,256]{2,1,0:T(8,128)S(1)}, f32[4,256,256]{2,1,0:T(8,128)S(1)}, f32[16,4,48,256]{3,2,1,0:T(8,128)}, f32[16,4,256,256]{3,2,1,...) while((s32[]{:T(128)}, f32[4,48,256]{2,1,0:T(8,128)S(1)}, ...), condition=%wide.region_1.2_spmd.clone, body=%wide.region_0.1_spmd.clone.sunk | while | flops 1703941 | bytes 11842204 | solution.py:55
  13.5 1.8 bitcast_dynamic-update-slice_fusion.7
  17.5 1.8 bitcast_dynamic-update-slice_fusion.7
  21.4 1.8 bitcast_dynamic-update-slice_fusion.7
  33.4 1.8 bitcast_dynamic-update-slice_fusion.7
  37.3 1.8 bitcast_dynamic-update-slice_fusion.7
  41.4 1.8 bitcast_dynamic-update-slice_fusion.7
  45.5 1.8 bitcast_dynamic-update-slice_fusion.7
  49.5 1.8 bitcast_dynamic-update-slice_fusion.7
  53.5 1.8 bitcast_dynamic-update-slice_fusion.7
  57.5 1.8 bitcast_dynamic-update-slice_fusion.7
  61.5 1.8 bitcast_dynamic-update-slice_fusion.7
  65.5 1.8 bitcast_dynamic-update-slice_fusion.7
  69.5 1.8 bitcast_dynamic-update-slice_fusion.7
  76.6 2.6 %while.62 = (s32[]{:T(128)}, f32[256,256]{0,1:T(8,128)S(1)}, f32[4,256,256]{2,1,0:T(8,128)S(1)}, s32[]{:T(128)}) while((s32[]{:T(128)}, f32[256,256]{0,1:T(8,128)S(1)}, f32[4,256,256]{2,1,0:T(8,128)S(1)}, s32[]{:T(128)}) %tuple.106), condition=%wide.region_3.4_spmd, body=%wide.region_2.3_spmd.sunk | while | flops 201326592 | bytes 1310777 | solution.py:66
  82.2 14.6 %all-gather.1 = f32[384,256]{1,0:T(8,128)} all-gather(f32[48,256]{1,0:T(8,128)S(1)} %get-tuple-element.156), channel_id=3, replica_groups=mesh['rows'=8,'chan'=32] {'rows'}, dimensions={0}, use_global_device_ids=true | all-gather | bytes 442368 | tf_op jit(solution)/shard_map/all_gather | solution.py:11
  96.7 12.7 %all-gather.4.cloned.1.call-done = f32[2048,256]{0,1:T(8,128)} async-done(((f32[256,256]{0,1:T(8,128)}), f32[2048,256]{0,1:T(8,128)}) %all-gather.4.cloned.1.call-update) | async-done | bytes 2097168 | tf_op jit(solution)/shard_map/all_gather | solution.py:11
  109.4 1.9 copy.54
  111.4 7.8 %while.63 = (s32[]{:T(128)}, f32[48,256]{1,0:T(8,128)S(1)}, s32[]{:T(128)}, f32[8,256,256]{2,1,0:T(8,128)S(1)}, f32[8,48,256]{2,1,0:T(8,128)}, /*index=5*/s32[]{:T(128)}, s32[]{:T(128)}, s32[]{:T(128)}) while((s32[]{:T(128)}, f32[48,256]{1,0:T(8,128)S(1)}, s32[]{:T(128)}, f32[8,256,256]{2,1,0:T(8,128)S(1)}, f32[8,48,256]{2,1,0:T(8,128)}, ...), condition=%wide.region_7.8_spmd, body=%wide.region_6.7_spmd.sunk | while | flops 37761028 | bytes 509047 | solution.py:19
  119.2 3.7 %while.64 = (s32[]{:T(128)}, f32[48,256]{1,0:T(8,128)S(1)}, f32[4,48,256]{2,1,0:T(8,128)}, f32[4,256,256]{2,1,0:T(8,128)S(1)}, f32[4,48,256]{2,1,0:T(8,128)S(1)}, /*index=5*/s32[]{:T(128)}) while((s32[]{:T(128)}, f32[48,256]{1,0:T(8,128)S(1)}, f32[4,48,256]{2,1,0:T(8,128)}, f32[4,256,256]{2,1,0:T(8,128)S(1)}, f32[4,48,256]{2,1,0:T(8,128)S(1)}, ...), condition=%wide.region_9.10_spmd, body=%wide.region_8.9_spmd.sunk | while | flops 37761024 | bytes 607813 | solution.py:77
  122.9 14.7 %bitcast_add_fusion.1 = f32[16,4,48,256]{3,2,0,1:T(8,128)S(1)} fusion(f32[16,4,48,256]{3,2,1,0:T(8,128)} %get-tuple-element.153, f32[16,4,256,256]{3,2,1,0:T(8,128)} %get-tuple-element.154, f32[4,48,256]{2,1,0:T(8,128)} %get-tuple-element.158), kind=kOutput, calls=%fused_computation.45 | convolution fusion | flops 2416705536 | bytes 23265280 | tf_op jit(solution)/shard_map/bcv,jbvw->jbcw/dot_general | solution.py:78
  139.2 49.8 %all_to_all.5 = bf16[32,2,48,256]{3,2,1,0:T(8,128)(2,1)S(1)} all-to-all(bf16[32,2,48,256]{3,2,1,0:T(8,128)(2,1)S(1)} %constant_dynamic-update-slice_fusion), channel_id=1, replica_groups=mesh['rows'=8,'chan'=32] {'chan'}, dimensions={0} | all-to-all | bytes 3145728 | tf_op jit(solution)/shard_map/all_to_all | solution.py:85
  189.1 2.7 %fusion.31 = bf16[2,1536,256]{1,2,0:T(8,128)(2,1)S(1)} fusion(bf16[2,1536,256]{2,1,0:T(8,128)(2,1)S(1)} %bitcast.259, bf16[1536,1536]{1,0:T(8,128)(2,1)S(1)} %bitcast.265), kind=kOutput, calls=%fused_computation.49 | convolution fusion | flops 2416705536 | bytes 7864320 | tf_op jit(solution)/shard_map/oc,rcw->row/dot_general | solution.py:81
  (219 shorter events, 63.2 us)
Async XLA Ops:
  6.5 102.9 %all-gather.4.cloned.1.call-start = ((), (), s32[]{:S(2)}) async-start(), calls=%async_computation.1 | async-start | bytes 2359296 | tf_op jit(solution)/shard_map/all_gather | solution.py:11
  7.6 3.6 %copy-start.2 = (f32[3,64,256]{2,1,0:T(8,128)S(1)}, f32[3,64,256]{2,1,0:T(8,128)}, u32[]{:S(2)}) copy-start(f32[3,64,256]{2,1,0:T(8,128)} %param.16) | copy-start | bytes 589828
  79.2 0.7 copy-start
  122.9 14.7 %copy-start.1 = (bf16[64,48,256]{2,1,0:T(8,128)(2,1)S(1)}, bf16[64,48,256]{2,1,0:T(8,128)(2,1)}, u32[]{:S(2)}) copy-start(bf16[64,48,256]{2,1,0:T(8,128)(2,1)} %param.18) | copy-start | bytes 4718596
  137.6 51.4 %slice-start = ((s8[4718592]{0:T(1024)(128)(4,1)}), s8[4194304]{0:T(1024)(128)(4,1)S(1)}, s32[]{:S(2)}) async-start(s8[4718592]{0:T(1024)(128)(4,1)} %bitcast.264), calls=%async_computation.2 | async-start | bytes 8388608
  139.0 50.1 %slice-start.1 = ((s8[4718592]{0:T(1024)(128)(4,1)}), s8[524288]{0:T(1024)(128)(4,1)S(1)}, s32[]{:S(2)}) async-start(s8[4718592]{0:T(1024)(128)(4,1)} %bitcast.264), calls=%async_computation.3 | async-start | bytes 1048576
Sparse Core Ops, SparseCore 0:
  80.1 29.3 all-gather.3
